TPU v7x, 32 devices: a whole 2x2x4 slice. The times are simulated.
32 devices in a mesh: prow: 4 (over y, x), pcol: 8 (over z, core).
Axes of the slice: x: 2, y: 2, z: 4, core: 2. Of those that a mesh axis runs over, the one named last changes fastest.
Arguments:
- rhs: bfloat16 [3, 8, 512, 128], P(None, 'pcol', 'prow'), may hold values from -6 to 6
- inverse_diagonal_blocks: bfloat16 [3, 8, 512, 512], P(None, 'pcol'), may hold values from -1 to 2, as said below
- offdiagonal_blocks: bfloat16 [2, 8, 4, 512, 512], P(None, 'pcol', 'prow'), may hold values from -0.09375 to 0.09375
- targets: int32 [2, 8, 4], P(None, 'pcol'), may hold values from 0 to 15, as said below
Outputs:
- solution: bfloat16 [3, 8, 512, 128], P(None, 'pcol', 'prow')
Inputs may be any that keep to these rules, and one draw needn't show every extreme that they name: For a supernode of level l the 4 entries of targets[l] are distinct and lie between l * 8 and (2) * 8 - 1, so they name supernodes of later levels only. Each block of inverse_diagonal_blocks is lower triangular.
All inputs are finite; a program needn't handle non-finite values.
Results may differ from a plain program's by a relative error of at most 0.014.
Values may be sent and summed in bfloat16 or wider, within the bound.
No kernel may reach another device: no remote copies, remote signals or barrier semaphores. Data moves between devices by JAX's collectives and lax.ppermute only.
A program may use at most 64 MiB of HBM per device.

v0:
```python
import jax
import jax.numpy as jnp
from jax import lax
from jax.sharding import PartitionSpec as P


def local(rhs, inverse_diagonal_blocks, offdiagonal_blocks, targets):
    levels = rhs.shape[0]
    per_group = rhs.shape[1]
    part_rows = rhs.shape[2]
    vector_count = rhs.shape[3]
    per_device = offdiagonal_blocks.shape[2]
    row_count = lax.axis_size("prow")
    level_size = per_group * lax.axis_size("pcol")
    upper_count = levels - 1
    row_index = lax.axis_index("prow")
    gathered_updates = jnp.zeros(
        (upper_count, row_count, level_size, part_rows, vector_count), jnp.float32
    )
    outputs = []
    for present_level in range(levels):
        remaining_rhs = rhs[present_level].astype(jnp.float32)
        if present_level > 0:
            due_block = gathered_updates[present_level - 1]
            reduced_once = lax.psum_scatter(
                due_block.astype(jnp.bfloat16), "pcol", scatter_dimension=1, tiled=True
            )
            arrived = lax.psum_scatter(
                reduced_once, "prow", scatter_dimension=0, tiled=True
            ).astype(jnp.float32)[0]
            remaining_rhs = remaining_rhs - arrived
        whole_block = lax.all_gather(remaining_rhs, "prow", axis=1, tiled=True)
        finished_unknowns = jnp.einsum(
            "rqe,rei->rqi",
            inverse_diagonal_blocks[present_level].astype(jnp.float32),
            whole_block,
            precision=lax.Precision.HIGHEST,
        ).astype(jnp.bfloat16)
        supernode_rows = lax.dynamic_slice_in_dim(
            finished_unknowns, row_index * part_rows, part_rows, 1
        )
        outputs.append(supernode_rows)
        if present_level < upper_count:
            products = jnp.einsum(
                "wsiq,wqm->wsim",
                offdiagonal_blocks[present_level],
                finished_unknowns,
                preferred_element_type=jnp.float32,
            )
            chosen = lax.dynamic_slice_in_dim(
                targets[present_level], row_index * per_device, per_device, 1
            )
            chosen = chosen.reshape(per_group * per_device)
            level_ids = chosen // level_size
            node_ids = chosen % level_size
            moved_rows = products.reshape(
                per_group * per_device, row_count, part_rows, vector_count
            )
            gathered_updates = gathered_updates.at[level_ids, :, node_ids].add(moved_rows)
    return jnp.stack(outputs)


def solution(mesh):
    in_specs = (
        P(None, "pcol", "prow", None),
        P(None, "pcol", None, None),
        P(None, "pcol", "prow", None, None),
        P(None, "pcol", None),
    )
    out_specs = P(None, "pcol", "prow", None)
    return jax.shard_map(local, mesh=mesh, in_specs=in_specs, out_specs=out_specs, check_vma=False)
```

profile of v0, /device:TPU:0, one launch (start us, length us, event | category | flops | bytes accessed | tf_op | source)
XLA Modules:
  0.0 184.7 jit_solution(10603757281627997184)
XLA Ops:
  6.5 0.7 fusion.22
  7.2 0.6 constant_dynamic-slice_fusion
  13.0 0.8 fusion.21
  13.8 10.5 %all-gather = f32[1,1,512,128]{3,2,1,0:T(8,128)S(1)} all-gather(f32[1,1,128,128]{3,2,1,0:T(8,128)S(1)} %get-tuple-element.35), channel_id=2, replica_groups=mesh['prow'=4,'pcol'=8] {'prow'}, dimensions={2}, use_global_device_ids=true | all-gather | bytes 327680 | tf_op jit(solution)/shard_map/all_gather | solution.py:32
  24.3 1.3 fusion.20
  25.7 1.6 convolution_convert_fusion.1
  27.4 1.4 and_reduce_fusion
  28.7 0.5 broadcast_in_dim.2
  29.2 0.9 fusion.1
  30.2 1.9 %copy-done = f32[2,4,8,128,128]{3,4,1,2,0:T(8,128)} copy-done((f32[2,4,8,128,128]{3,4,1,2,0:T(8,128)}, f32[2,4,8,128,128]{3,4,1,2,0:T(8,128)S(1)}, u32[]{:S(2)}) %copy-start) | copy-done | bytes 4194328
  32.1 1.1 fusion.5
  33.3 33.0 %reduce-scatter.15.cloned.1.call-done = bf16[4,1,128,128]{2,3,0,1:T(8,128)(2,1)} async-done(((bf16[4,8,128,128]{2,3,0,1:T(8,128)(2,1)}), bf16[4,1,128,128]{2,3,0,1:T(8,128)(2,1)}) %reduce-scatter.15.cloned.1.call-update) | async-done | bytes 131088 | tf_op jit(solution)/shard_map/reduce_scatter | solution.py:25
  66.5 24.9 %reduce-scatter.19.cloned.1.call-done = bf16[1,1,128,128]{2,3,0,1:T(8,128)(2,1)} async-done(((bf16[4,1,128,128]{2,3,0,1:T(8,128)(2,1)}), bf16[1,1,128,128]{2,3,0,1:T(8,128)(2,1)}) %reduce-scatter.19.cloned.1.call-update) | async-done | bytes 32784
  91.4 0.8 convert_subtract_fusion.1
  92.2 10.0 %all-gather.1 = f32[1,1,512,128]{2,3,0,1:T(8,128)S(1)} all-gather(f32[1,1,128,128]{2,3,0,1:T(8,128)S(1)} %convert_subtract_fusion.1), channel_id=3, replica_groups=mesh['prow'=4,'pcol'=8] {'prow'}, dimensions={2}, use_global_device_ids=true | all-gather | bytes 327680 | tf_op jit(solution)/shard_map/all_gather | solution.py:32
  102.2 0.7 convolution_convert_fusion
  102.9 2.6 %fusion.4 = f32[2,4,8,128,128]{3,4,1,2,0:T(8,128)} fusion(f32[2,4,8,128,128]{3,4,1,2,0:T(8,128)} %copy-done, s32[]{:T(128)} %bitcast.16, s32[]{:T(128)} %bitcast.17, bf16[4,128,512]{2,1,0:T(8,128)(2,1)S(1)} %bitcast.81, bf16[128,512]{1,0:T(8,128)(2,1)S(1)} %convolution_convert_fusion, pred[]{:T(512)} %get-tuple-element.29), kind=kOutput, calls=%fused_computation.8 | convolution fusion | flops 67239936 | bytes 1181184 | tf_op jit(solution)/shard_map/wsiq,wqm->wsim/dot_general | solution.py:44
  105.5 2.7 %fusion.6 = bf16[4,8,128,128]{2,3,0,1:T(8,128)(2,1)} fusion(f32[2,4,8,128,128]{3,4,1,2,0:T(8,128)} %fusion.4), kind=kLoop, calls=%fused_computation.12 | loop fusion | bytes 2097152 | tf_op jit(solution)/shard_map/convert_element_type | solution.py:26
  108.2 32.7 %reduce-scatter.17.cloned.1.call-done = bf16[4,1,128,128]{2,3,0,1:T(8,128)(2,1)} async-done(((bf16[4,8,128,128]{2,3,0,1:T(8,128)(2,1)}), bf16[4,1,128,128]{2,3,0,1:T(8,128)(2,1)}) %reduce-scatter.17.cloned.1.call-update) | async-done | bytes 131088 | tf_op jit(solution)/shard_map/reduce_scatter | solution.py:25
  141.2 24.6 %reduce-scatter.21.cloned.1.call-done = bf16[1,1,128,128]{2,3,0,1:T(8,128)(2,1)} async-done(((bf16[4,1,128,128]{2,3,0,1:T(8,128)(2,1)}), bf16[1,1,128,128]{2,3,0,1:T(8,128)(2,1)}) %reduce-scatter.21.cloned.1.call-update) | async-done | bytes 32784
  165.9 0.8 convert_subtract_fusion
  166.7 10.0 %all-gather.2 = f32[1,1,512,128]{2,3,0,1:T(8,128)S(1)} all-gather(f32[1,1,128,128]{2,3,0,1:T(8,128)S(1)} %convert_subtract_fusion), channel_id=4, replica_groups=mesh['prow'=4,'pcol'=8] {'prow'}, dimensions={2}, use_global_device_ids=true | all-gather | bytes 327680 | tf_op jit(solution)/shard_map/all_gather | solution.py:32
  176.7 0.7 fusion.7
  177.4 0.8 copy.18
  (20 shorter events, 0.7 us)
Async XLA Ops:
  6.5 59.8 %reduce-scatter.15.cloned.1.call-start = ((), (), s32[]{:S(2)}) async-start(), calls=%async_computation.4 | async-start | bytes 1179648 | tf_op jit(solution)/shard_map/reduce_scatter | solution.py:25
  28.7 73.4 %copy-start.1 = (bf16[3,1,512,512]{3,2,1,0:T(8,128)(2,1)S(1)}, bf16[3,1,512,512]{3,2,1,0:T(8,128)(2,1)}, u32[]{:S(2)}) copy-start(bf16[3,1,512,512]{3,2,1,0:T(8,128)(2,1)} %param.9) | copy-start | bytes 4718596
  30.2 1.9 %copy-start = (f32[2,4,8,128,128]{3,4,1,2,0:T(8,128)}, f32[2,4,8,128,128]{3,4,1,2,0:T(8,128)S(1)}, u32[]{:S(2)}) copy-start(f32[2,4,8,128,128]{3,4,1,2,0:T(8,128)S(1)} %fusion.1) | copy-start | bytes 12582916
  33.3 58.1 %reduce-scatter.19.cloned.1.call-start = ((), (), s32[]{:S(2)}) async-start(), calls=%async_computation.6 | async-start | bytes 163840
  66.4 74.6 %reduce-scatter.17.cloned.1.call-start = ((), (), s32[]{:S(2)}) async-start(), calls=%async_computation.5 | async-start | bytes 1179648 | tf_op jit(solution)/shard_map/reduce_scatter | solution.py:25
  108.2 57.7 %reduce-scatter.21.cloned.1.call-start = ((), (), s32[]{:S(2)}) async-start(), calls=%async_computation.7 | async-start | bytes 163840
Sparse Core Ops, SparseCore 0:
  33.4 32.8 reduce-scatter.14
  69.1 22.3 reduce-scatter.18
  108.3 32.5 reduce-scatter.16
  143.5 22.3 reduce-scatter.20
where the time goes:
time: 185 us
  waiting for transfers between devices  115 us (62%)
  blocking collectives  30.4 us (16%)
  between operations  18.4 us (10%)
  local copies, waits for them, and re-layouts  10.1 us (5%)
  matrix products  6.49 us (4%)
  other arithmetic  3.72 us (2%)
    reduce_scatter x2, waiting for transfers between devices, local(): lax.psum_scatter(due_block.astype(jnp.bfloat16), 'pcol', scatter_dimensio...  65.7 us
    unnamed x6, waiting for transfers between devices  49.6 us
    all_gather x3, blocking collectives, local(): whole_block = lax.all_gather(remaining_rhs, 'prow', axis=1, tiled=True)  30.4 us
    convert_element_type x2, local copies, waits for them, and re-layouts, local(): due_block.astype(jnp.bfloat16)  3.85 us
  transfers between devices with their start and end apart: 4, of which 4 were waited for; matrix products, arithmetic and copies ran while one was open for 0% of the time, Pallas kernels for 0%

commit v1 on v0

--- a/solution.py
+++ b/solution.py
@@ -2,6 +2,17 @@
 import jax.numpy as jnp
 from jax import lax
 from jax.sharding import PartitionSpec as P
+
+
+def gather_around(value, axis, dim):
+    ways = lax.axis_size(axis)
+    pieces = [value]
+    for far in range(1, ways):
+        pieces.append(
+            lax.ppermute(pieces[far - 1], axis, [(d, (d - 1) % ways) for d in range(ways)])
+        )
+    line = jnp.concatenate(pieces, axis=dim)
+    return jnp.roll(line, lax.axis_index(axis) * value.shape[dim], axis=dim)
 
 
 def local(rhs, inverse_diagonal_blocks, offdiagonal_blocks, targets):
@@ -29,7 +40,7 @@
                 reduced_once, "prow", scatter_dimension=0, tiled=True
             ).astype(jnp.float32)[0]
             remaining_rhs = remaining_rhs - arrived
-        whole_block = lax.all_gather(remaining_rhs, "prow", axis=1, tiled=True)
+        whole_block = gather_around(remaining_rhs, "prow", 1)
         finished_unknowns = jnp.einsum(
             "rqe,rei->rqi",
             inverse_diagonal_blocks[present_level].astype(jnp.float32),

time: 185 us -> 195 us (1.054)
  blocking collectives: 30.4 us -> 0 us
  starting transfers between devices: 0.12 us -> 21 us
  waiting for transfers between devices: 115 us -> 135 us
    all_gather x3 -> x0, blocking collectives: 30.4 us -> none  [local(): whole_block = lax.all_gather(remaining_rhs, 'prow', axis=1, tiled=True)]
    ppermute x0 -> x9, starting transfers between devices: none -> 20.8 us  [gather_around(): lax.ppermute(pieces[far - 1], axis, [(d, (d - 1) % ways) for d in range(w...]
    ppermute x0 -> x9, waiting for transfers between devices: none -> 18.1 us  [gather_around(): lax.ppermute(pieces[far - 1], axis, [(d, (d - 1) % ways) for d in range(w...]
  transfers between devices with their start and end apart: 4 -> 13, of which waited for: 4 -> 12; matrix products, arithmetic and copies ran while one was open for 0% -> 2% of each run, Pallas kernels for 0% -> 0%
where the time goes in v1:
time: 195 us
  waiting for transfers between devices  135 us (69%)
  starting transfers between devices  21 us (11%)
  between operations  18.4 us (9%)
  local copies, waits for them, and re-layouts  10 us (5%)
  matrix products  6.93 us (4%)
  other arithmetic  3.71 us (2%)
    reduce_scatter x2, waiting for transfers between devices, local(): lax.psum_scatter(due_block.astype(jnp.bfloat16), 'pcol', scatter_dimensio...  66.6 us
    unnamed x6, waiting for transfers between devices  49.8 us
    ppermute x9, starting transfers between devices, gather_around(): lax.ppermute(pieces[far - 1], axis, [(d, (d - 1) % ways) for d in range(w...  20.8 us
    ppermute x9, waiting for transfers between devices, gather_around(): lax.ppermute(pieces[far - 1], axis, [(d, (d - 1) % ways) for d in range(w...  18.1 us
  transfers between devices with their start and end apart: 13, of which 12 were waited for; matrix products, arithmetic and copies ran while one was open for 2% of the time, Pallas kernels for 0%

profile of v1, /device:TPU:0, one launch (start us, length us, event | category | flops | bytes accessed | tf_op | source)
XLA Modules:
  0.0 194.6 jit_solution(10775570923343016875)
XLA Ops:
  7.3 4.0 %collective-permute-start = (f32[1,128,128]{2,1,0:T(8,128)S(1)}, f32[1,128,128]{2,1,0:T(8,128)S(1)}, u32[]{:S(2)}, u32[]{:S(2)}) collective-permute-start(f32[1,128,128]{2,1,0:T(8,128)S(1)} %get-tuple-element.36), channel_id=1, source_target_pairs={{0,24},{8,0},{16,8},{24,16},{1,25},{9,1},{17,9},{25,17},{2,26},{10... | collective-permute-start | bytes 196616 | tf_op jit(solution)/shard_map/ppermute | solution.py:12
  13.2 3.3 %collective-permute-start.1 = (f32[1,128,128]{2,1,0:T(8,128)S(1)}, f32[1,128,128]{2,1,0:T(8,128)S(1)}, u32[]{:S(2)}, u32[]{:S(2)}) collective-permute-start(f32[1,128,128]{2,1,0:T(8,128)S(1)} %collective-permute-done), channel_id=1, source_target_pairs={{0,24},{8,0},{16,8},{24,16},{1,25},{9,1},{17,9},{25,17},{2,26},{10... | collective-permute-start | bytes 196616 | tf_op jit(solution)/shard_map/ppermute | solution.py:12
  23.1 1.4 and_reduce_fusion
  24.5 2.9 %collective-permute-done.2 = f32[1,128,128]{2,1,0:T(8,128)S(1)} collective-permute-done((f32[1,128,128]{2,1,0:T(8,128)S(1)}, f32[1,128,128]{2,1,0:T(8,128)S(1)}, u32[]{:S(2)}, u32[]{:S(2)}) %collective-permute-start.2) | collective-permute-done | bytes 65568 | tf_op jit(solution)/shard_map/ppermute | solution.py:12
  27.4 2.2 %convolution_convert_fusion.1 = bf16[128,512]{1,0:T(8,128)(2,1)S(1)} fusion(bf16[3,1,512,512]{3,2,1,0:T(8,128)(2,1)} %param.11, s32[]{:T(128)S(6)} %select_n.64, f32[1,128,128]{2,1,0:T(8,128)S(1)} %get-tuple-element.36, f32[1,128,128]{2,1,0:T(8,128)S(1)} %collective-permute-done, f32[1,128,128]{2,1,0:T(8,128)S(1)} %collective-permute-done.1, ...), kind=kOutput, calls=%fused_computation.10 | convolution fusion | flops 403177472 | bytes 917508 | tf_op jit(solution)/shard_map/rqe,rei->rqi/dot_general | solution.py:44
  31.1 1.9 copy-done
  34.2 32.4 %reduce-scatter.15.cloned.1.call-done = bf16[4,1,128,128]{2,3,0,1:T(8,128)(2,1)} async-done(((bf16[4,8,128,128]{2,3,0,1:T(8,128)(2,1)}), bf16[4,1,128,128]{2,3,0,1:T(8,128)(2,1)}) %reduce-scatter.15.cloned.1.call-update) | async-done | bytes 131088 | tf_op jit(solution)/shard_map/reduce_scatter | solution.py:36
  66.8 24.9 %reduce-scatter.19.cloned.1.call-done = bf16[1,1,128,128]{2,3,0,1:T(8,128)(2,1)} async-done(((bf16[4,1,128,128]{2,3,0,1:T(8,128)(2,1)}), bf16[1,1,128,128]{2,3,0,1:T(8,128)(2,1)}) %reduce-scatter.19.cloned.1.call-update) | async-done | bytes 32784
  92.5 1.5 collective-permute-start.3
  94.0 2.8 %collective-permute-done.3 = f32[1,128,128]{1,2,0:T(8,128)S(1)} collective-permute-done((f32[1,128,128]{1,2,0:T(8,128)S(1)}, f32[1,128,128]{1,2,0:T(8,128)S(1)}, u32[]{:S(2)}, u32[]{:S(2)}) %collective-permute-start.3) | collective-permute-done | bytes 65568 | tf_op jit(solution)/shard_map/ppermute | solution.py:12
  96.9 2.4 %collective-permute-start.4 = (f32[1,128,128]{1,2,0:T(8,128)S(1)}, f32[1,128,128]{1,2,0:T(8,128)S(1)}, u32[]{:S(2)}, u32[]{:S(2)}) collective-permute-start(f32[1,128,128]{1,2,0:T(8,128)S(1)} %collective-permute-done.3), channel_id=1, source_target_pairs={{0,24},{8,0},{16,8},{24,16},{1,25},{9,1},{17,9},{25,17},{2,26},{10... | collective-permute-start | bytes 196616 | tf_op jit(solution)/shard_map/ppermute | solution.py:12
  99.2 2.2 %collective-permute-done.4 = f32[1,128,128]{1,2,0:T(8,128)S(1)} collective-permute-done((f32[1,128,128]{1,2,0:T(8,128)S(1)}, f32[1,128,128]{1,2,0:T(8,128)S(1)}, u32[]{:S(2)}, u32[]{:S(2)}) %collective-permute-start.4) | collective-permute-done | bytes 65568 | tf_op jit(solution)/shard_map/ppermute | solution.py:12
  101.5 2.9 %collective-permute-start.5 = (f32[1,128,128]{1,2,0:T(8,128)S(1)}, f32[1,128,128]{1,2,0:T(8,128)S(1)}, u32[]{:S(2)}, u32[]{:S(2)}) collective-permute-start(f32[1,128,128]{1,2,0:T(8,128)S(1)} %collective-permute-done.4), channel_id=1, source_target_pairs={{0,24},{8,0},{16,8},{24,16},{1,25},{9,1},{17,9},{25,17},{2,26},{10... | collective-permute-start | bytes 196616 | tf_op jit(solution)/shard_map/ppermute | solution.py:12
  104.4 2.2 %collective-permute-done.5 = f32[1,128,128]{1,2,0:T(8,128)S(1)} collective-permute-done((f32[1,128,128]{1,2,0:T(8,128)S(1)}, f32[1,128,128]{1,2,0:T(8,128)S(1)}, u32[]{:S(2)}, u32[]{:S(2)}) %collective-permute-start.5) | collective-permute-done | bytes 65568 | tf_op jit(solution)/shard_map/ppermute | solution.py:12
  107.3 2.5 %fusion.4 = f32[2,4,8,128,128]{3,4,1,2,0:T(8,128)} fusion(f32[2,4,8,128,128]{3,4,1,2,0:T(8,128)} %copy-done, s32[]{:T(128)} %bitcast.20, s32[]{:T(128)} %bitcast.21, bf16[4,128,512]{2,1,0:T(8,128)(2,1)S(1)} %bitcast.90, bf16[128,512]{1,0:T(8,128)(2,1)S(1)} %convolution_convert_fusion, pred[]{:T(512)} %get-tuple-element.30), kind=kOutput, calls=%fused_computation.8 | convolution fusion | flops 67239936 | bytes 1181184 | tf_op jit(solution)/shard_map/wsiq,wqm->wsim/dot_general | solution.py:55
  109.8 2.7 %fusion.6 = bf16[4,8,128,128]{2,3,0,1:T(8,128)(2,1)} fusion(f32[2,4,8,128,128]{3,4,1,2,0:T(8,128)} %fusion.4), kind=kLoop, calls=%fused_computation.12 | loop fusion | bytes 2097152 | tf_op jit(solution)/shard_map/convert_element_type | solution.py:37
  112.6 34.2 %reduce-scatter.17.cloned.1.call-done = bf16[4,1,128,128]{2,3,0,1:T(8,128)(2,1)} async-done(((bf16[4,8,128,128]{2,3,0,1:T(8,128)(2,1)}), bf16[4,1,128,128]{2,3,0,1:T(8,128)(2,1)}) %reduce-scatter.17.cloned.1.call-update) | async-done | bytes 131088 | tf_op jit(solution)/shard_map/reduce_scatter | solution.py:36
  146.9 24.8 %reduce-scatter.21.cloned.1.call-done = bf16[1,1,128,128]{2,3,0,1:T(8,128)(2,1)} async-done(((bf16[4,1,128,128]{2,3,0,1:T(8,128)(2,1)}), bf16[1,1,128,128]{2,3,0,1:T(8,128)(2,1)}) %reduce-scatter.21.cloned.1.call-update) | async-done | bytes 32784
  172.5 1.5 collective-permute-start.6
  174.0 2.8 %collective-permute-done.6 = f32[1,128,128]{1,2,0:T(8,128)S(1)} collective-permute-done((f32[1,128,128]{1,2,0:T(8,128)S(1)}, f32[1,128,128]{1,2,0:T(8,128)S(1)}, u32[]{:S(2)}, u32[]{:S(2)}) %collective-permute-start.6) | collective-permute-done | bytes 65568 | tf_op jit(solution)/shard_map/ppermute | solution.py:12
  176.8 2.4 %collective-permute-start.7 = (f32[1,128,128]{1,2,0:T(8,128)S(1)}, f32[1,128,128]{1,2,0:T(8,128)S(1)}, u32[]{:S(2)}, u32[]{:S(2)}) collective-permute-start(f32[1,128,128]{1,2,0:T(8,128)S(1)} %collective-permute-done.6), channel_id=1, source_target_pairs={{0,24},{8,0},{16,8},{24,16},{1,25},{9,1},{17,9},{25,17},{2,26},{10... | collective-permute-start | bytes 196616 | tf_op jit(solution)/shard_map/ppermute | solution.py:12
  179.2 2.2 %collective-permute-done.7 = f32[1,128,128]{1,2,0:T(8,128)S(1)} collective-permute-done((f32[1,128,128]{1,2,0:T(8,128)S(1)}, f32[1,128,128]{1,2,0:T(8,128)S(1)}, u32[]{:S(2)}, u32[]{:S(2)}) %collective-permute-start.7) | collective-permute-done | bytes 65568 | tf_op jit(solution)/shard_map/ppermute | solution.py:12
  181.4 2.9 %collective-permute-start.8 = (f32[1,128,128]{1,2,0:T(8,128)S(1)}, f32[1,128,128]{1,2,0:T(8,128)S(1)}, u32[]{:S(2)}, u32[]{:S(2)}) collective-permute-start(f32[1,128,128]{1,2,0:T(8,128)S(1)} %collective-permute-done.7), channel_id=1, source_target_pairs={{0,24},{8,0},{16,8},{24,16},{1,25},{9,1},{17,9},{25,17},{2,26},{10... | collective-permute-start | bytes 196616 | tf_op jit(solution)/shard_map/ppermute | solution.py:12
  184.4 2.2 %collective-permute-done.8 = f32[1,128,128]{1,2,0:T(8,128)S(1)} collective-permute-done((f32[1,128,128]{1,2,0:T(8,128)S(1)}, f32[1,128,128]{1,2,0:T(8,128)S(1)}, u32[]{:S(2)}, u32[]{:S(2)}) %collective-permute-start.8) | collective-permute-done | bytes 65568 | tf_op jit(solution)/shard_map/ppermute | solution.py:12
  (34 shorter events, 10.7 us)
Async XLA Ops:
  6.5 60.1 %reduce-scatter.15.cloned.1.call-start = ((), (), s32[]{:S(2)}) async-start(), calls=%async_computation.4 | async-start | bytes 1179648 | tf_op jit(solution)/shard_map/reduce_scatter | solution.py:36
  7.3 5.9 %collective-permute-start = (f32[1,128,128]{2,1,0:T(8,128)S(1)}, f32[1,128,128]{2,1,0:T(8,128)S(1)}, u32[]{:S(2)}, u32[]{:S(2)}) collective-permute-start(f32[1,128,128]{2,1,0:T(8,128)S(1)} %get-tuple-element.36), channel_id=1, source_target_pairs={{0,24},{8,0},{16,8},{24,16},{1,25},{9,1},{17,9},{25,17},{2,26},{10... | collective-permute-start | bytes 196616 | tf_op jit(solution)/shard_map/ppermute | solution.py:12
  13.2 9.9 %collective-permute-start.1 = (f32[1,128,128]{2,1,0:T(8,128)S(1)}, f32[1,128,128]{2,1,0:T(8,128)S(1)}, u32[]{:S(2)}, u32[]{:S(2)}) collective-permute-start(f32[1,128,128]{2,1,0:T(8,128)S(1)} %collective-permute-done), channel_id=1, source_target_pairs={{0,24},{8,0},{16,8},{24,16},{1,25},{9,1},{17,9},{25,17},{2,26},{10... | collective-permute-start | bytes 196616 | tf_op jit(solution)/shard_map/ppermute | solution.py:12
  23.1 4.3 %collective-permute-start.2 = (f32[1,128,128]{2,1,0:T(8,128)S(1)}, f32[1,128,128]{2,1,0:T(8,128)S(1)}, u32[]{:S(2)}, u32[]{:S(2)}) collective-permute-start(f32[1,128,128]{2,1,0:T(8,128)S(1)} %collective-permute-done.1), channel_id=1, source_target_pairs={{0,24},{8,0},{16,8},{24,16},{1,25},{9,1},{17,9},{25,17},{2,26},{10... | collective-permute-start | bytes 196616 | tf_op jit(solution)/shard_map/ppermute | solution.py:12
  29.6 77.0 %copy-start.1 = (bf16[3,1,512,512]{3,2,1,0:T(8,128)(2,1)S(1)}, bf16[3,1,512,512]{3,2,1,0:T(8,128)(2,1)}, u32[]{:S(2)}) copy-start(bf16[3,1,512,512]{3,2,1,0:T(8,128)(2,1)} %param.11) | copy-start | bytes 4718596
  31.1 1.9 %copy-start = (f32[2,4,8,128,128]{3,4,1,2,0:T(8,128)}, f32[2,4,8,128,128]{3,4,1,2,0:T(8,128)S(1)}, u32[]{:S(2)}) copy-start(f32[2,4,8,128,128]{3,4,1,2,0:T(8,128)S(1)} %fusion.1) | copy-start | bytes 12582916
  34.2 57.6 %reduce-scatter.19.cloned.1.call-start = ((), (), s32[]{:S(2)}) async-start(), calls=%async_computation.6 | async-start | bytes 163840
  66.7 80.1 %reduce-scatter.17.cloned.1.call-start = ((), (), s32[]{:S(2)}) async-start(), calls=%async_computation.5 | async-start | bytes 1179648 | tf_op jit(solution)/shard_map/reduce_scatter | solution.py:36
  92.5 4.3 %collective-permute-start.3 = (f32[1,128,128]{1,2,0:T(8,128)S(1)}, f32[1,128,128]{1,2,0:T(8,128)S(1)}, u32[]{:S(2)}, u32[]{:S(2)}) collective-permute-start(f32[1,128,128]{1,2,0:T(8,128)S(1)} %subtract_bitcast_fusion.1), channel_id=1, source_target_pairs={{0,24},{8,0},{16,8},{24,16},{1,25},{9,1},{17,9},{25,17},{2,26},{10... | collective-permute-start | bytes 196616 | tf_op jit(solution)/shard_map/ppermute | solution.py:12
  96.9 4.6 %collective-permute-start.4 = (f32[1,128,128]{1,2,0:T(8,128)S(1)}, f32[1,128,128]{1,2,0:T(8,128)S(1)}, u32[]{:S(2)}, u32[]{:S(2)}) collective-permute-start(f32[1,128,128]{1,2,0:T(8,128)S(1)} %collective-permute-done.3), channel_id=1, source_target_pairs={{0,24},{8,0},{16,8},{24,16},{1,25},{9,1},{17,9},{25,17},{2,26},{10... | collective-permute-start | bytes 196616 | tf_op jit(solution)/shard_map/ppermute | solution.py:12
  101.5 5.2 %collective-permute-start.5 = (f32[1,128,128]{1,2,0:T(8,128)S(1)}, f32[1,128,128]{1,2,0:T(8,128)S(1)}, u32[]{:S(2)}, u32[]{:S(2)}) collective-permute-start(f32[1,128,128]{1,2,0:T(8,128)S(1)} %collective-permute-done.4), channel_id=1, source_target_pairs={{0,24},{8,0},{16,8},{24,16},{1,25},{9,1},{17,9},{25,17},{2,26},{10... | collective-permute-start | bytes 196616 | tf_op jit(solution)/shard_map/ppermute | solution.py:12
  112.5 59.2 %reduce-scatter.21.cloned.1.call-start = ((), (), s32[]{:S(2)}) async-start(), calls=%async_computation.7 | async-start | bytes 163840
  172.5 4.3 %collective-permute-start.6 = (f32[1,128,128]{1,2,0:T(8,128)S(1)}, f32[1,128,128]{1,2,0:T(8,128)S(1)}, u32[]{:S(2)}, u32[]{:S(2)}) collective-permute-start(f32[1,128,128]{1,2,0:T(8,128)S(1)} %subtract_bitcast_fusion), channel_id=1, source_target_pairs={{0,24},{8,0},{16,8},{24,16},{1,25},{9,1},{17,9},{25,17},{2,26},{10... | collective-permute-start | bytes 196616 | tf_op jit(solution)/shard_map/ppermute | solution.py:12
  176.8 4.6 %collective-permute-start.7 = (f32[1,128,128]{1,2,0:T(8,128)S(1)}, f32[1,128,128]{1,2,0:T(8,128)S(1)}, u32[]{:S(2)}, u32[]{:S(2)}) collective-permute-start(f32[1,128,128]{1,2,0:T(8,128)S(1)} %collective-permute-done.6), channel_id=1, source_target_pairs={{0,24},{8,0},{16,8},{24,16},{1,25},{9,1},{17,9},{25,17},{2,26},{10... | collective-permute-start | bytes 196616 | tf_op jit(solution)/shard_map/ppermute | solution.py:12
  181.4 5.2 %collective-permute-start.8 = (f32[1,128,128]{1,2,0:T(8,128)S(1)}, f32[1,128,128]{1,2,0:T(8,128)S(1)}, u32[]{:S(2)}, u32[]{:S(2)}) collective-permute-start(f32[1,128,128]{1,2,0:T(8,128)S(1)} %collective-permute-done.7), channel_id=1, source_target_pairs={{0,24},{8,0},{16,8},{24,16},{1,25},{9,1},{17,9},{25,17},{2,26},{10... | collective-permute-start | bytes 196616 | tf_op jit(solution)/shard_map/ppermute | solution.py:12
Sparse Core Ops, SparseCore 0:
  34.3 32.3 reduce-scatter.14
  69.4 22.3 reduce-scatter.18
  112.6 34.0 reduce-scatter.16
  149.4 22.3 reduce-scatter.20
